TPU v7x, 128 devices: a whole 4x4x4 slice. The times are simulated.
128 devices in a mesh: lat: 16 (over z, x_hi, core), lon: 8 (over y, x_lo).
Axes of the slice: x: 4 (x_hi: 2, x_lo: 2; x = x_hi * 2 + x_lo), y: 4, z: 4, core: 2. Of those that a mesh axis runs over, the one named last changes fastest.
Arguments:
- thermal_anomaly: float32 [40, 128, 12288], P(None, 'lat', 'lon'), may hold values from -6 to 6
- saltiness_anomaly: float32 [40, 128, 12288], P(None, 'lat', 'lon'), may hold values from -6 to 6
- easterly_flow: float32 [40, 128, 12288], P(None, 'lat', 'lon'), may hold values from -3 to 3
- poleward_flow: float32 [40, 128, 12288], P(None, 'lat', 'lon'), may hold values from -3 to 3
- planetary_spin: float32 [128], P('lat'), may hold values from -1.5 to 1.5
- marine_indicator: int32 [40, 128, 12288], P(None, 'lat', 'lon'), may hold values 0 or 1
- active_strata: int32 [128, 12288], P('lat', 'lon'), may hold values from 1 to 40
Outputs:
- temperature_next: float32 [40, 128, 12288], P(None, 'lat', 'lon')
- salinity_next: float32 [40, 128, 12288], P(None, 'lat', 'lon')
- easterly_flow_after: float32 [40, 128, 12288], P(None, 'lat', 'lon')
- meridional_next: float32 [40, 128, 12288], P(None, 'lat', 'lon')
- spectral_capture: bfloat16 [2, 10, 32, 3072], P(None, None, 'lat')
All inputs are finite; a program needn't handle non-finite values. No bound on the sum of `marine_indicator` on one device may be relied on, other than what follows from the above.
Results may differ from a plain program's by a relative error of at most 0.003.
Values may be sent and summed in bfloat16 or wider, within the bound.
A program may use at most 192 MiB of HBM per device.

v0:
```python
import functools
import math

import jax
import jax.numpy as jnp
from jax import lax
from jax.experimental import pallas as pl
from jax.experimental.pallas import tpu as pltpu
from jax.sharding import PartitionSpec as P

MESH = pl.DeviceIdType.MESH
BUOY_SALT = 0.25 * 0.25 * 0.8
BUOY_HEAT = 0.25 * 0.25 * 0.2
CARRY = 0.2 * 0.25
MIX = 0.2 * 0.8
VERT = 0.1
FLAT = math.sqrt(1.0 / 8.0)
WAVE = [math.sqrt(2.0 / 8.0) * math.cos(math.pi * (2 * n + 1) / 16.0) for n in range(8)]
ROWS = 8
LANES = 128
BLOCK = 8


def pairwise_sum(parts):
    while len(parts) > 1:
        parts = [sum(parts[i : i + 2][1:], parts[i]) for i in range(0, len(parts), 2)]
    return parts[0]


def table_value(freq, place):
    wave = jnp.full(freq.shape, WAVE[0], jnp.float32)
    for n in range(1, 8):
        wave = jnp.where(place == n, WAVE[n], wave)
    return jnp.where(freq == 0, FLAT, wave)


def fluxes(near, far, both, pairs):
    t = CARRY * (near + far)
    a = both * (t + MIX)
    b = both * (t - MIX)
    return [a * q + b * n for q, n in pairs]


def step_kernel(
    n_lat,
    n_lon,
    spin,
    heat_hbm,
    salt_hbm,
    east_hbm,
    pole_hbm,
    sea_hbm,
    depth_hbm,
    heat_out,
    salt_out,
    east_out,
    pole_out,
    coef_out,
    heat,
    salt,
    east,
    pole,
    sea,
    depth,
    wet,
    press,
    row_send,
    from_south,
    from_north,
    edge_box,
    side_send,
    from_west,
    from_east,
    halo_box,
    halo_cols,
    upward,
    tower,
    lane_table,
    row_table,
    stack,
    coef_send,
    load_sem,
    depth_sem,
    row_send_sem,
    south_sem,
    north_sem,
    side_send_sem,
    west_sem,
    east_sem,
    coef_send_sem,
    coef_sem,
):
    chunks = depth.shape[0] // ROWS
    cols = chunks * LANES
    tall = chunks * ROWS
    total = press.shape[0]
    blocks = total // (tall * BLOCK)
    slab = BLOCK * ROWS
    la = lax.axis_index("lat")
    lo = lax.axis_index("lon")
    above = {"lat": lax.rem(la + 1, n_lat)}
    below = {"lat": lax.rem(la + n_lat - 1, n_lat)}
    right = {"lon": lax.rem(lo + 1, n_lon)}
    left = {"lon": lax.rem(lo + n_lon - 1, n_lon)}
    has_above = la < n_lat - 1
    has_below = la > 0

    fields = ((heat_hbm, heat), (salt_hbm, salt), (sea_hbm, sea), (east_hbm, east), (pole_hbm, pole))

    def load(i, b):
        hbm, vmem = fields[i]
        part = pl.ds(pl.multiple_of(b * BLOCK * tall, BLOCK * tall), BLOCK * tall)
        return pltpu.make_async_copy(hbm.at[part], vmem.at[part], load_sem.at[i, b])

    depth_load = pltpu.make_async_copy(depth_hbm, depth, depth_sem)
    depth_load.start()
    for b in range(blocks):
        for i in range(len(fields)):
            load(i, b).start()

    barrier = pltpu.get_barrier_semaphore()
    peers = [above, below] + [{"lon": lax.rem(lo + d, n_lon)} for d in range(1, n_lon)]
    for peer in peers:
        pl.semaphore_signal(barrier, inc=1, device_id=peer, device_id_type=MESH)

    lane = lax.broadcasted_iota(jnp.int32, (ROWS, LANES), 1)
    row = lax.broadcasted_iota(jnp.int32, (ROWS, LANES), 0)
    spin_half = jnp.full((ROWS, LANES), 0.5 * spin[0], jnp.float32)
    for j in range(1, ROWS):
        spin_half = jnp.where(row == j, 0.5 * spin[j], spin_half)
    zero = jnp.zeros((ROWS, LANES), jnp.float32)

    deep, wide = lane_table.shape
    n = lax.broadcasted_iota(jnp.int32, (deep, wide), 0)
    o = lax.broadcasted_iota(jnp.int32, (deep, wide), 1)
    lane_table[...] = jnp.where(n // 8 == o // 2, table_value(o % 2, n % 8), 0.0)
    n = lax.broadcasted_iota(jnp.int32, row_table.shape, 1)
    o = lax.broadcasted_iota(jnp.int32, row_table.shape, 0)
    row_table[...] = jnp.where(n // 8 == o // 2, table_value(o % 2, n % 8), 0.0)
    edge_box[...] = jnp.zeros_like(edge_box)
    halo_box[...] = jnp.zeros_like(halo_box)
    upward[...] = jnp.zeros_like(upward)
    tower[...] = jnp.zeros_like(tower)
    for f in (heat, salt, wet):
        f[total:, :] = jnp.zeros((tall, LANES), jnp.float32)

    @pl.when(la == 0)
    def _():
        from_south[...] = jnp.zeros_like(from_south)

    @pl.when(la == n_lat - 1)
    def _():
        from_north[...] = jnp.zeros_like(from_north)

    depth_load.wait()
    pl.semaphore_wait(barrier, len(peers))

    def at(k, c):
        return pl.ds(pl.multiple_of(k * tall, tall) + c * ROWS, ROWS)

    def lines(b, j, c):
        return pl.ds(pl.multiple_of(b * BLOCK * tall, BLOCK * tall) + (c * ROWS + j), BLOCK, stride=tall)

    def row_copy(b, side):
        return pltpu.make_async_remote_copy(
            src_ref=row_send.at[side, b],
            dst_ref=(from_north if side == 0 else from_south).at[b],
            send_sem=row_send_sem.at[side, b],
            recv_sem=(north_sem if side == 0 else south_sem).at[b],
            device_id=below if side == 0 else above,
            device_id_type=MESH,
        )

    def side_copy(b, side):
        return pltpu.make_async_remote_copy(
            src_ref=side_send.at[b],
            dst_ref=(from_east if side == 0 else from_west).at[b],
            send_sem=side_send_sem.at[side, b],
            recv_sem=(east_sem if side == 0 else west_sem).at[b],
            device_id=left if side == 0 else right,
            device_id_type=MESH,
        )

    def coef_copy(b, d):
        place = pl.ds(pl.multiple_of(lo * (cols // 4), LANES), cols // 4)
        return pltpu.make_async_remote_copy(
            src_ref=coef_send.at[b],
            dst_ref=coef_out.at[:, pl.ds(2 * b, 2), :, place],
            send_sem=coef_send_sem.at[b, d],
            recv_sem=coef_sem.at[b, d],
            device_id={"lon": lax.rem(lo + d, n_lon)},
            device_id_type=MESH,
        )

    def first(b, running):
        for i in range(len(fields)):
            load(i, b).wait()

        def level(i, running):
            k = b * BLOCK + i
            out = []
            for c in range(chunks):
                here = at(k, c)
                w = jnp.where(k < depth[c * ROWS : (c + 1) * ROWS, :], sea[here, :], 0).astype(jnp.float32)
                d = w * (BUOY_SALT * salt[here, :] - BUOY_HEAT * heat[here, :])
                s = running[c] + d
                wet[here, :] = w
                press[here, :] = s - 0.5 * d
                out.append(s)
            return tuple(out)

        running = lax.fori_loop(0, BLOCK, level, running)

        for i in range(BLOCK):
            for side in range(2):
                here = at(b * BLOCK + i, 0 if side == 0 else chunks - 1)
                p = press[here, :]
                w = wet[here, :]
                flow = east[here, :] + spin_half * pole[here, :]
                if side == 0:
                    part = w * (flow - pltpu.roll(p, LANES - 1, 1))
                else:
                    part = w * (flow + pltpu.roll(p, 1, 1))
                box = zero
                for f, v in enumerate((heat[here, :], salt[here, :], w, part, p)):
                    shift = f if side == 0 else f + 1
                    v = pltpu.roll(v, shift, 1) if shift else v
                    box = jnp.where(lane == f, v, box)
                edge_box[side * slab + i * ROWS : side * slab + (i + 1) * ROWS, :] = box
        side_send[b] = edge_box[...].T[:ROWS, :]
        side_copy(b, 0).start()
        side_copy(b, 1).start()

        for side in range(2):
            j, inner = (0, 1) if side == 0 else (ROWS - 1, ROWS - 2)
            f = 0.5 * spin[j]
            for c in range(chunks):
                ch = slice(c * LANES, (c + 1) * LANES)

                def line(ref, j):
                    return ref[lines(b, j, c), :]

                w = line(wet, j)
                p = line(press, inner)
                flow = line(pole, j) - f * line(east, j)
                part = w * (flow - p) if side == 0 else w * (flow + p)
                row_send[side, b, 0:16, ch] = jnp.concatenate([line(heat, j), line(salt, j)], 0).astype(jnp.bfloat16)
                row_send[side, b, 16:32, ch] = jnp.concatenate([w, part], 0).astype(jnp.bfloat16)

        @pl.when(has_below)
        def _():
            row_copy(b, 0).start()

        @pl.when(has_above)
        def _():
            row_copy(b, 1).start()

        return running

    lax.fori_loop(0, blocks, first, (zero,) * chunks)

    def second(b, _):
        side_copy(b, 0).wait_recv()
        side_copy(b, 1).wait_recv()
        halo_box[0:ROWS, :] = jnp.where(lane < slab, from_east[b], from_west[b])
        halo_cols[...] = halo_box[...].T

        def level(i, _):
            k = b * BLOCK + i
            over_east = halo_cols[pl.ds(pl.multiple_of(i * ROWS, ROWS), ROWS), :]
            over_west = halo_cols[pl.ds(pl.multiple_of(slab + i * ROWS, ROWS), ROWS), :]
            last = LANES - 1

            def chunk(ref, c):
                return ref[at(k, c), :]

            def to_last(f):
                return pltpu.roll(over_east, last - f, 1)

            def to_first(f):
                return pltpu.roll(over_west, LANES - f, 1) if f else over_west

            def ahead(turned, c):
                return jnp.where(lane == last, turned[c + 1], turned[c])

            p = [chunk(press, c) for c in range(chunks)]
            w = [chunk(wet, c) for c in range(chunks)]
            p_ahead = [pltpu.roll(x, last, 1) for x in p] + [to_last(4)]
            p_back = [to_first(4)] + [pltpu.roll(x, 1, 1) for x in p]
            u, v = [], []
            for c in range(chunks):
                e, n = chunk(east, c), chunk(pole, c)
                dx = ahead(p_ahead, c) - jnp.where(lane == 0, p_back[c], p_back[c + 1])
                u.append(w[c] * (e + (spin_half * n - dx)))
                north = jnp.where(row == ROWS - 1, 0.0, pltpu.roll(p[c], ROWS - 1, 0))
                south = jnp.where(row == 0, 0.0, pltpu.roll(p[c], 1, 0))
                v.append(w[c] * (n - (spin_half * e + (north - south))))
                east_out[at(k, c), :] = u[c]
                pole_out[at(k, c), :] = v[c]

            q = [[chunk(f, c) for c in range(chunks)] for f in (heat, salt)]
            w_ahead = [pltpu.roll(x, last, 1) for x in w] + [to_last(2)]
            u_ahead = [pltpu.roll(x, last, 1) for x in u]
            u_ahead.append(to_last(3) + to_last(2) * p[chunks - 1])
            q_ahead = [
                [pltpu.roll(x, last, 1) for x in q[t]] + [to_last(t)] for t in range(2)
            ]
            w_out = to_first(2)
            u_out = to_first(3) - w_out * p[0]
            flux_back = fluxes(
                u_out, u[0], w_out * w[0], [(to_first(t), q[t][0]) for t in range(2)]
            )
            for c in range(chunks):
                flux = fluxes(
                    u[c],
                    ahead(u_ahead, c),
                    w[c] * ahead(w_ahead, c),
                    [(q[t][c], ahead(q_ahead[t], c)) for t in range(2)],
                )
                turned = [pltpu.roll(x, 1, 1) for x in flux]
                flux_n = fluxes(
                    v[c],
                    pltpu.roll(v[c], ROWS - 1, 0),
                    w[c] * jnp.where(row == ROWS - 1, 0.0, pltpu.roll(w[c], ROWS - 1, 0)),
                    [(q[t][c], pltpu.roll(q[t][c], ROWS - 1, 0)) for t in range(2)],
                )
                both = VERT * (w[c] * wet[at(k + 1, c), :])
                for t, (f, out) in enumerate(((heat, heat_out), (salt, salt_out))):
                    above_q = f[at(k + 1, c), :]
                    rise = both * (above_q - q[t][c])
                    held = slice((t * chunks + c) * ROWS, (t * chunks + c + 1) * ROWS)
                    gain = rise - upward[held, :]
                    upward[held, :] = rise
                    dx = flux[t] - jnp.where(lane == 0, flux_back[t], turned[t])
                    dy = flux_n[t] - pltpu.roll(flux_n[t], 1, 0)
                    out[at(k, c), :] = w[c] * ((q[t][c] + gain) - (dx + dy))
                flux_back = turned
            return 0

        lax.fori_loop(0, BLOCK, level, 0)
        return 0

    lax.fori_loop(0, blocks, second, 0)

    def third(b, _):
        for side in range(2):
            got = from_north if side == 0 else from_south
            j, inner = (ROWS - 1, ROWS - 2) if side == 0 else (0, 1)

            @pl.when(has_above if side == 0 else has_below)
            def _():
                row_copy(b, side).wait_recv()

            for c in range(chunks):
                ch = slice(c * LANES, (c + 1) * LANES)

                def line(ref, j):
                    return ref[lines(b, j, c), :]

                tracers = got[b, 0:16, ch].astype(jnp.float32)
                rest = got[b, 16:32, ch].astype(jnp.float32)
                q_far = (tracers[0:8], tracers[8:16])
                w_far, v_far = rest[0:8], rest[8:16]
                d = w_far * (BUOY_SALT * q_far[1] - BUOY_HEAT * q_far[0])
                s = d
                for gap in (1, 2, 4):
                    s = s + jnp.where(row >= gap, pltpu.roll(s, gap, 0), 0.0)
                held = slice((side * chunks + c) * ROWS, (side * chunks + c + 1) * ROWS)
                s = s + tower[held, :]
                tower[held, :] = jnp.broadcast_to(s[BLOCK - 1 : BLOCK, :], (BLOCK, LANES))
                p_far = s - 0.5 * d
                w, w_in = line(wet, j), line(wet, inner)
                p = line(press, j)
                if side == 0:
                    change = -(w * p_far)
                    v_far = v_far + w_far * p
                else:
                    change = w * p_far
                    v_far = v_far - w_far * p
                v = line(pole_out, j) + change
                pole_out[lines(b, j, c), :] = v
                t = CARRY * (v + v_far)
                both = w * w_far
                up = both * (t + MIX)
                down = both * (t - MIX)
                inside = (w * w_in) * (CARRY * change)
                for f, out, far in ((heat, heat_out, q_far[0]), (salt, salt_out, q_far[1])):
                    q, q_in = line(f, j), line(f, inner)
                    shift = inside * (q + q_in)
                    if side == 0:
                        edge = shift - (up * q + down * far)
                        back = -shift
                    else:
                        edge = (up * far + down * q) - shift
                        back = shift
                    out[lines(b, j, c), :] = line(out, j) + edge
                    out[lines(b, inner, c), :] = line(out, inner) + back

        groups = chunks // 4
        for t, f in enumerate((heat_out, salt_out)):
            for c in range(chunks):
                x = [f[at(b * BLOCK + i, c), :] for i in range(BLOCK)]
                add = [x[i] + x[BLOCK - 1 - i] for i in range(BLOCK // 2)]
                dif = [WAVE[i] * (x[i] - x[BLOCK - 1 - i]) for i in range(BLOCK // 2)]
                g, s = c // 4, slice((c % 4) * LANES, (c % 4 + 1) * LANES)
                base = g * 4 * ROWS + t * 2 * ROWS
                stack[base : base + ROWS, s] = FLAT * pairwise_sum(add)
                stack[base + ROWS : base + 2 * ROWS, s] = pairwise_sum(dif)
        short = jnp.dot(
            stack[...], lane_table[...], precision=lax.Precision.HIGHEST, preferred_element_type=jnp.float32
        )
        for g in range(groups):
            done = jnp.dot(
                row_table[...],
                short[g * 4 * ROWS : (g + 1) * 4 * ROWS, :],
                precision=lax.Precision.HIGHEST,
                preferred_element_type=jnp.float32,
            )
            for t in range(2):
                for p in range(2):
                    part = done[4 * t + 2 * p : 4 * t + 2 * p + 2, :].astype(jnp.bfloat16)
                    coef_send[b, t, p, :, g * LANES : (g + 1) * LANES] = part
                    place = pl.ds(pl.multiple_of(lo * (cols // 4) + g * LANES, LANES), LANES)
                    coef_out[t, 2 * b + p, :, place] = part
        for d in range(1, n_lon):
            coef_copy(b, d).start()
        return 0

    lax.fori_loop(0, blocks, third, 0)

    def finish(b, _):
        for d in range(1, n_lon):
            coef_copy(b, d).wait()
        side_copy(b, 0).wait_send()
        side_copy(b, 1).wait_send()

        @pl.when(has_below)
        def _():
            row_copy(b, 0).wait_send()

        @pl.when(has_above)
        def _():
            row_copy(b, 1).wait_send()

        return 0

    lax.fori_loop(0, blocks, finish, 0)


def on_device(n_lat, n_lon, heat, salt, east, pole, spin, sea, depth):
    levels, rows, cols = heat.shape
    chunks, blocks = cols // LANES, levels // BLOCK
    tall = chunks * rows
    total = levels * tall
    field = pltpu.VMEM((total, LANES), jnp.float32)
    longer = pltpu.VMEM((total + tall, LANES), jnp.float32)
    dma = pltpu.SemaphoreType.DMA
    hbm = pl.BlockSpec(memory_space=pl.ANY)

    def tiled(x):
        x = x.reshape(x.shape[:-1] + (chunks, LANES))
        return jnp.swapaxes(x, -3, -2).reshape(-1, LANES)

    def whole(x):
        return jnp.swapaxes(x.reshape(levels, chunks, rows, LANES), 1, 2).reshape(levels, rows, cols)

    outs = pl.pallas_call(
        functools.partial(step_kernel, n_lat, n_lon),
        out_shape=[OUT_SPACE((total, LANES), jnp.float32)] * 4
        + [OUT_SPACE((2, 2 * blocks, 2, n_lon * cols // 4), jnp.bfloat16)],
        in_specs=[pl.BlockSpec(memory_space=pltpu.SMEM)] + [hbm] * 6,
        out_specs=[pl.BlockSpec(memory_space=pltpu.VMEM)] * 5,
        scratch_shapes=[
            longer,
            longer,
            field,
            field,
            pltpu.VMEM((total, LANES), jnp.int32),
            pltpu.VMEM((tall, LANES), jnp.int32),
            longer,
            field,
            pltpu.VMEM((2, blocks, 4 * BLOCK, cols), jnp.bfloat16),
            pltpu.VMEM((blocks, 4 * BLOCK, cols), jnp.bfloat16),
            pltpu.VMEM((blocks, 4 * BLOCK, cols), jnp.bfloat16),
            pltpu.VMEM((LANES, LANES), jnp.float32),
            pltpu.VMEM((blocks, ROWS, LANES), jnp.float32),
            pltpu.VMEM((blocks, ROWS, LANES), jnp.float32),
            pltpu.VMEM((blocks, ROWS, LANES), jnp.float32),
            pltpu.VMEM((LANES, LANES), jnp.float32),
            pltpu.VMEM((LANES, LANES), jnp.float32),
            pltpu.VMEM((2 * tall, LANES), jnp.float32),
            pltpu.VMEM((2 * tall, LANES), jnp.float32),
            pltpu.VMEM((4 * LANES, LANES), jnp.float32),
            pltpu.VMEM((ROWS, 4 * ROWS), jnp.float32),
            pltpu.VMEM((cols // (4 * LANES) * 4 * ROWS, 4 * LANES), jnp.float32),
            pltpu.VMEM((blocks, 2, 2, 2, cols // 4), jnp.bfloat16),
            dma((5, blocks)),
            dma,
            dma((2, blocks)),
            dma((blocks,)),
            dma((blocks,)),
            dma((2, blocks)),
            dma((blocks,)),
            dma((blocks,)),
            dma((blocks, n_lon)),
            dma((blocks, n_lon)),
        ],
        compiler_params=pltpu.CompilerParams(collective_id=0, has_side_effects=True, vmem_limit_bytes=28 << 20),
        name="ocean_step",
    )(
        spin, tiled(heat), tiled(salt), tiled(east), tiled(pole), tiled(sea), tiled(depth)
    )
    return tuple(whole(x) for x in outs[:4]) + (outs[4],)


OUT_SPACE = jax.ShapeDtypeStruct


def solution(mesh):
    field = P(None, "lat", "lon")
    return jax.shard_map(
        functools.partial(on_device, mesh.shape["lat"], mesh.shape["lon"]),
        mesh=mesh,
        in_specs=(field, field, field, field, P("lat"), field, P("lat", "lon")),
        out_specs=(field, field, field, field, P(None, None, "lat", None)),
        check_vma=False,
    )
```

profile of v0, /device:TPU:0, one launch (start us, length us, event | category | flops | bytes accessed | tf_op | source)
XLA Modules:
  0.0 56.7 jit_solution(161484840684643809)
XLA Ops:
  0.6 0.0 copy-start
  0.6 1.5 %copy-done = f32[40,8,1536]{2,1,0:T(8,128)S(1)} copy-done((f32[40,8,1536]{2,1,0:T(8,128)S(1)}, f32[40,8,1536]{2,1,0:T(8,128)}, u32[]{:S(2)}) %copy-start) | copy-done | bytes 1966104
  2.2 0.0 copy-start.1
  2.2 1.5 %copy-done.1 = f32[40,8,1536]{2,1,0:T(8,128)S(1)} copy-done((f32[40,8,1536]{2,1,0:T(8,128)S(1)}, f32[40,8,1536]{2,1,0:T(8,128)}, u32[]{:S(2)}) %copy-start.1) | copy-done | bytes 1966104
  3.7 0.0 copy-start.2
  3.7 1.5 %copy-done.2 = f32[40,8,1536]{2,1,0:T(8,128)S(1)} copy-done((f32[40,8,1536]{2,1,0:T(8,128)S(1)}, f32[40,8,1536]{2,1,0:T(8,128)}, u32[]{:S(2)}) %copy-start.2) | copy-done | bytes 1966104
  5.3 0.0 copy-start.3
  5.3 1.5 %copy-done.3 = f32[40,8,1536]{2,1,0:T(8,128)S(1)} copy-done((f32[40,8,1536]{2,1,0:T(8,128)S(1)}, f32[40,8,1536]{2,1,0:T(8,128)}, u32[]{:S(2)}) %copy-start.3) | copy-done | bytes 1966104
  6.8 0.0 copy-start.4
  6.8 1.5 %copy-done.4 = s32[40,8,1536]{2,1,0:T(8,128)S(1)} copy-done((s32[40,8,1536]{2,1,0:T(8,128)S(1)}, s32[40,8,1536]{2,1,0:T(8,128)}, u32[]{:S(2)}) %copy-start.4) | copy-done | bytes 1966104
  8.4 0.0 copy-start.5
  8.4 0.8 %copy-done.5 = s32[8,1536]{1,0:T(8,128)S(1)} copy-done((s32[8,1536]{1,0:T(8,128)S(1)}, s32[8,1536]{1,0:T(8,128)}, u32[]{:S(2)}) %copy-start.5) | copy-done | bytes 49176
  9.2 0.0 copy-start.6
  9.2 0.7 %copy-done.6 = f32[8]{0:T(128)S(1)} copy-done((f32[8]{0:T(128)S(1)}, f32[8]{0:T(128)}, u32[]{:S(2)}) %copy-start.6) | copy-done | bytes 56
  9.8 41.1 %ocean_step.1 = (f32[3840,128]{1,0:T(8,128)S(1)}, f32[3840,128]{1,0:T(8,128)S(1)}, f32[3840,128]{1,0:T(8,128)S(1)}, f32[3840,128]{1,0:T(8,128)S(1)}, bf16[2,10,2,3072]{3,2,1,0:T(2,128)(2,1)S(1)}) custom-call(f32[8]{0:T(128)S(1)} %copy-done.6, f32[3840,128]{1,0:T(8,128)S(1)} %bitcast.50, f32[3840,128]{1,0:T(8,128)S(1)} %bitcast.51, f32[3840,128]{1,0:T(8,128)S(1)} %bitcast.52, ...), custom_call_target="tpu_custom_call" | custom-call | tf_op jit(solution)/shard_map/ocean_step/pallas_call | solution.py:467
  50.9 1.3 %copy.17 = f32[40,8,1536]{2,1,0:T(8,128)} copy(f32[40,8,1536]{2,1,0:T(8,128)S(1)} %bitcast.58) | data formatting | bytes 3932160
  52.2 1.3 %copy.18 = f32[40,8,1536]{2,1,0:T(8,128)} copy(f32[40,8,1536]{2,1,0:T(8,128)S(1)} %bitcast.57) | data formatting | bytes 3932160
  53.5 1.3 %copy.19 = f32[40,8,1536]{2,1,0:T(8,128)} copy(f32[40,8,1536]{2,1,0:T(8,128)S(1)} %bitcast.56) | data formatting | bytes 3932160
  54.7 1.3 %copy.20 = f32[40,8,1536]{2,1,0:T(8,128)} copy(f32[40,8,1536]{2,1,0:T(8,128)S(1)} %bitcast.55) | data formatting | bytes 3932160
  56.0 0.7 %copy.21 = bf16[2,10,2,3072]{3,2,1,0:T(2,128)(2,1)} copy(bf16[2,10,2,3072]{3,2,1,0:T(2,128)(2,1)S(1)} %get-tuple-element.24) | data formatting | bytes 491520
Async XLA Ops:
  0.6 1.5 %copy-start = (f32[40,8,1536]{2,1,0:T(8,128)S(1)}, f32[40,8,1536]{2,1,0:T(8,128)}, u32[]{:S(2)}) copy-start(f32[40,8,1536]{2,1,0:T(8,128)} %param.7) | copy-start | bytes 5898244
  2.2 1.5 %copy-start.1 = (f32[40,8,1536]{2,1,0:T(8,128)S(1)}, f32[40,8,1536]{2,1,0:T(8,128)}, u32[]{:S(2)}) copy-start(f32[40,8,1536]{2,1,0:T(8,128)} %param.8) | copy-start | bytes 5898244
  3.7 1.5 %copy-start.2 = (f32[40,8,1536]{2,1,0:T(8,128)S(1)}, f32[40,8,1536]{2,1,0:T(8,128)}, u32[]{:S(2)}) copy-start(f32[40,8,1536]{2,1,0:T(8,128)} %param.9) | copy-start | bytes 5898244
  5.3 1.5 %copy-start.3 = (f32[40,8,1536]{2,1,0:T(8,128)S(1)}, f32[40,8,1536]{2,1,0:T(8,128)}, u32[]{:S(2)}) copy-start(f32[40,8,1536]{2,1,0:T(8,128)} %param.10) | copy-start | bytes 5898244
  6.8 1.5 %copy-start.4 = (s32[40,8,1536]{2,1,0:T(8,128)S(1)}, s32[40,8,1536]{2,1,0:T(8,128)}, u32[]{:S(2)}) copy-start(s32[40,8,1536]{2,1,0:T(8,128)} %param.12) | copy-start | bytes 5898244
  8.4 0.8 %copy-start.5 = (s32[8,1536]{1,0:T(8,128)S(1)}, s32[8,1536]{1,0:T(8,128)}, u32[]{:S(2)}) copy-start(s32[8,1536]{1,0:T(8,128)} %param.13) | copy-start | bytes 147460
  9.2 0.7 %copy-start.6 = (f32[8]{0:T(128)S(1)}, f32[8]{0:T(128)}, u32[]{:S(2)}) copy-start(f32[8]{0:T(128)} %spin.1) | copy-start | bytes 100
where the time goes:
time: 57 us; the launch traced here: 56.7 us
  Pallas kernels  41.1 us (72%)
  local copies, waits for them, and re-layouts  14.9 us (26%)
  between operations  0.66 us (1%)
    pallas_call x1, Pallas kernels, on_device(): pl.pallas_call(functools.partial(step_kernel, n_lat, n_lon), out_shape=[O...  41.1 us
    unnamed x19, local copies, waits for them, and re-layouts  14.9 us

commit v1 on v0

v1 whole, which is shorter than its diff:
```python
import functools
import math

import jax
import jax.numpy as jnp
from jax import lax
from jax.experimental import pallas as pl
from jax.experimental.pallas import tpu as pltpu
from jax.sharding import PartitionSpec as P

MESH = pl.DeviceIdType.MESH
BUOY_SALT = 0.25 * 0.25 * 0.8
BUOY_HEAT = 0.25 * 0.25 * 0.2
CARRY = 0.2 * 0.25
MIX = 0.2 * 0.8
VERT = 0.1
FLAT = math.sqrt(1.0 / 8.0)
WAVE = [math.sqrt(2.0 / 8.0) * math.cos(math.pi * (2 * n + 1) / 16.0) for n in range(8)]
ROWS = 8
LANES = 128
BLOCK = 8


def pairwise_sum(parts):
    while len(parts) > 1:
        parts = [sum(parts[i : i + 2][1:], parts[i]) for i in range(0, len(parts), 2)]
    return parts[0]


def table_value(freq, place):
    wave = jnp.full(freq.shape, WAVE[0], jnp.float32)
    for n in range(1, 8):
        wave = jnp.where(place == n, WAVE[n], wave)
    return jnp.where(freq == 0, FLAT, wave)


def fluxes(near, far, both, pairs):
    t = CARRY * (near + far)
    a = both * (t + MIX)
    b = both * (t - MIX)
    return [a * q + b * n for q, n in pairs]


REVERSED = (0, 4, 2, 6, 1, 5, 3, 7)


def edge_rows(x, row):
    y = [x[i] for i in REVERSED]
    ends = (row == 0) | (row == ROWS - 1)
    outer = ends | (row == 3) | (row == 4)
    even = lax.rem(row, 2) == 0
    pairs = [jnp.where(ends, y[i], pltpu.roll(y[i + 1], 4, 0)) for i in range(0, 8, 2)]
    low, high = (jnp.where(outer, pairs[i], pltpu.roll(pairs[i + 1], 2, 0)) for i in (0, 2))
    high = pltpu.roll(high, 1, 0)
    return jnp.where(even, low, high), pltpu.roll(jnp.where(even, high, low), 1, 0)


def step_kernel(
    n_lat,
    n_lon,
    spin_hbm,
    heat_hbm,
    salt_hbm,
    east_hbm,
    pole_hbm,
    sea_hbm,
    depth_hbm,
    heat_out,
    salt_out,
    east_out,
    pole_out,
    coef_out,
    heat,
    salt,
    east,
    pole,
    sea,
    depth,
    wet,
    press,
    row_send,
    from_south,
    from_north,
    edge_box,
    side_send,
    from_west,
    from_east,
    halo_box,
    halo_cols,
    upward,
    below_sum,
    tower,
    own_edge,
    edge_value,
    lane_table,
    stack,
    coef_send,
    spin,
    load_sem,
    depth_sem,
    spin_sem,
    row_send_sem,
    south_sem,
    north_sem,
    side_send_sem,
    west_sem,
    east_sem,
    coef_send_sem,
    coef_sem,
    partner_sem,
    coef_keep_sem,
):
    chunks = depth.shape[0] // ROWS
    cols = chunks * LANES
    tall = chunks * ROWS
    total = press.shape[0]
    blocks = total // (tall * BLOCK)
    slab = BLOCK * ROWS
    la = lax.axis_index("lat")
    lo = lax.axis_index("lon")
    above = {"lat": lax.rem(la + 1, n_lat)}
    below = {"lat": lax.rem(la + n_lat - 1, n_lat)}
    right = {"lon": lax.rem(lo + 1, n_lon)}
    left = {"lon": lax.rem(lo + n_lon - 1, n_lon)}
    has_above = la < n_lat - 1
    has_below = la > 0

    fields = ((heat_hbm, heat), (salt_hbm, salt), (sea_hbm, sea), (east_hbm, east), (pole_hbm, pole))

    def load(i, b):
        hbm, vmem = fields[i]
        part = pl.ds(pl.multiple_of(b * BLOCK * tall, BLOCK * tall), BLOCK * tall)
        return pltpu.make_async_copy(hbm.at[part], vmem.at[part], load_sem.at[b])

    barrier = pltpu.get_barrier_semaphore()
    peers = [above, below] + [{"lon": lax.rem(lo + d, n_lon)} for d in range(1, n_lon)]
    for peer in peers:
        pl.semaphore_signal(barrier, inc=1, device_id=peer, device_id_type=MESH)

    depth_load = pltpu.make_async_copy(depth_hbm, depth, depth_sem)
    depth_load.start()
    spin_load = pltpu.make_async_copy(spin_hbm, spin, spin_sem)
    spin_load.start()
    for b in range(blocks):
        for i in range(len(fields)):
            load(i, b).start()

    lane = lax.broadcasted_iota(jnp.int32, (ROWS, LANES), 1)
    row = lax.broadcasted_iota(jnp.int32, (ROWS, LANES), 0)
    zero = jnp.zeros((ROWS, LANES), jnp.float32)

    deep = lane_table.shape[0]
    n = lax.broadcasted_iota(jnp.int32, (deep, LANES), 0)
    o = lax.broadcasted_iota(jnp.int32, (deep, LANES), 1)
    table = jnp.where(n // 8 == o // 2, table_value(o % 2, n % 8), 0.0)
    high = table.astype(jnp.bfloat16)
    lane_table[:, :LANES] = high
    lane_table[:, LANES:] = (table - high.astype(jnp.float32)).astype(jnp.bfloat16)
    row_wave = table_value(jnp.ones_like(row), row)
    edge_box[...] = jnp.zeros_like(edge_box)
    halo_box[...] = jnp.zeros_like(halo_box)
    upward[...] = jnp.zeros_like(upward)
    below_sum[...] = jnp.zeros_like(below_sum)
    tower[...] = jnp.zeros_like(tower)
    for f in (heat, salt, wet):
        f[total:, :] = jnp.zeros((tall, LANES), jnp.float32)

    @pl.when(la == 0)
    def _():
        from_south[...] = jnp.zeros_like(from_south)

    @pl.when(la == n_lat - 1)
    def _():
        from_north[...] = jnp.zeros_like(from_north)

    spin_load.wait()
    spin_half = jnp.full((ROWS, LANES), 0.5 * spin[0], jnp.float32)
    for j in range(1, ROWS):
        spin_half = jnp.where(row == j, 0.5 * spin[j], spin_half)
    depth_load.wait()
    pl.semaphore_wait(barrier, len(peers))

    def at(k, c):
        return pl.ds(pl.multiple_of(k * tall, tall) + c * ROWS, ROWS)

    def tile(i):
        return pl.ds(pl.multiple_of(i * ROWS, ROWS), ROWS)

    def own(b, side, f, c):
        return tile(((b * 2 + side) * 5 + f) * chunks + c)

    def row_copy(b, side):
        return pltpu.make_async_remote_copy(
            src_ref=row_send.at[side, b],
            dst_ref=(from_north if side == 0 else from_south).at[b],
            send_sem=row_send_sem.at[side],
            recv_sem=(north_sem if side == 0 else south_sem).at[b],
            device_id=below if side == 0 else above,
            device_id_type=MESH,
        )

    def side_copy(b, side):
        return pltpu.make_async_remote_copy(
            src_ref=side_send.at[b],
            dst_ref=(from_east if side == 0 else from_west).at[b],
            send_sem=side_send_sem.at[side],
            recv_sem=(east_sem if side == 0 else west_sem).at[b],
            device_id=left if side == 0 else right,
            device_id_type=MESH,
        )

    partner = lo + 1 - 2 * lax.rem(lo, 2)
    width = cols // 4

    def place(owner):
        return pl.ds(pl.multiple_of(owner * width, LANES), width)

    def coef_copy(b, kind, dy=0):
        ahead_y = lax.rem(lo + 2 * dy, n_lon)
        target = (partner, ahead_y, ahead_y, lax.rem(partner + 2 * dy, n_lon))[kind]
        owner = partner if kind == 2 else lo
        there = coef_out.at[:, pl.ds(2 * b, 2), :, place(owner)]
        return pltpu.make_async_remote_copy(
            src_ref=there if kind == 2 else coef_send.at[b],
            dst_ref=there,
            send_sem=coef_send_sem,
            recv_sem=partner_sem.at[b] if kind == 0 else coef_sem,
            device_id={"lon": target},
            device_id_type=MESH,
        )

    def coef_keep(b):
        here = coef_out.at[:, pl.ds(2 * b, 2), :, place(lo)]
        return pltpu.make_async_copy(coef_send.at[b], here, coef_keep_sem)

    turns = range(1, n_lon // 2)

    def first(b, _):
        pltpu.make_async_copy(heat_hbm, heat.at[pl.ds(0, total)], load_sem.at[b]).wait()
        for c in range(chunks):
            deep = depth[c * ROWS : (c + 1) * ROWS, :]
            s = below_sum[c * ROWS : (c + 1) * ROWS, :]
            cells = []
            for i in range(BLOCK):
                k = b * BLOCK + i
                here = at(k, c)
                w = jnp.where(k < deep, sea[here, :], 0).astype(jnp.float32)
                t, q = heat[here, :], salt[here, :]
                d = w * (BUOY_SALT * q - BUOY_HEAT * t)
                s = s + d
                p = s - 0.5 * d
                wet[here, :] = w
                press[here, :] = p
                inner = jnp.where(row == 0, -pltpu.roll(p, ROWS - 1, 0), pltpu.roll(p, 1, 0))
                cells.append((t, q, w, w * ((pole[here, :] - spin_half * east[here, :]) + inner), p))
            below_sum[c * ROWS : (c + 1) * ROWS, :] = s
            edges = [edge_rows(x, row) for x in zip(*cells)]
            ch = slice(c * LANES, (c + 1) * LANES)
            for side in range(2):
                for f in range(5):
                    own_edge[own(b, side, f, c), :] = edges[f][side]
                for f in (0, 2):
                    pair = jnp.concatenate([edges[f][side], edges[f + 1][side]], 0)
                    row_send[side, b, 8 * f : 8 * f + 16, ch] = pair.astype(jnp.bfloat16)

        @pl.when(has_below)
        def _():
            row_copy(b, 0).start()

        @pl.when(has_above)
        def _():
            row_copy(b, 1).start()

        for i in range(BLOCK):
            for side in range(2):
                here = at(b * BLOCK + i, 0 if side == 0 else chunks - 1)
                p = press[here, :]
                w = wet[here, :]
                flow = east[here, :] + spin_half * pole[here, :]
                if side == 0:
                    part = w * (flow - pltpu.roll(p, LANES - 1, 1))
                else:
                    part = w * (flow + pltpu.roll(p, 1, 1))
                box = zero
                for f, v in enumerate((heat[here, :], salt[here, :], w, part, p)):
                    shift = f if side == 0 else f + 1
                    v = pltpu.roll(v, shift, 1) if shift else v
                    box = jnp.where(lane == f, v, box)
                edge_box[side * slab + i * ROWS : side * slab + (i + 1) * ROWS, :] = box
        side_send[b] = edge_box[...].T[:ROWS, :]
        side_copy(b, 0).start()
        side_copy(b, 1).start()
        return 0

    lax.fori_loop(0, blocks, first, 0)

    def second(b, _):
        side_copy(b, 0).wait_recv()
        side_copy(b, 1).wait_recv()
        halo_box[0:ROWS, :] = jnp.where(lane < slab, from_east[b], from_west[b])
        halo_cols[...] = halo_box[...].T

        for side in range(2):
            got = from_south if side == 0 else from_north

            @pl.when(has_below if side == 0 else has_above)
            def _():
                row_copy(b, 1 - side).wait_recv()

            for c in range(chunks):
                ch = slice(c * LANES, (c + 1) * LANES)
                q0, q1, w, part, p = (own_edge[own(b, side, f, c), :] for f in range(5))
                tracers = got[b, 0:16, ch].astype(jnp.float32)
                rest = got[b, 16:32, ch].astype(jnp.float32)
                far0, far1, w_far, v_far = tracers[0:8], tracers[8:16], rest[0:8], rest[8:16]
                d = w_far * (BUOY_SALT * far1 - BUOY_HEAT * far0)
                s = d
                for gap in (1, 2, 4):
                    s = s + jnp.where(row >= gap, pltpu.roll(s, gap, 0), 0.0)
                held = slice((side * chunks + c) * ROWS, (side * chunks + c + 1) * ROWS)
                s = s + tower[held, :]
                tower[held, :] = jnp.broadcast_to(s[BLOCK - 1 : BLOCK, :], (BLOCK, LANES))
                p_far = s - 0.5 * d
                if side == 0:
                    v = part + w * p_far
                    v_far = v_far - w_far * p
                    flux = fluxes(v_far, v, w * w_far, [(far0, q0), (far1, q1)])
                else:
                    v = part - w * p_far
                    v_far = v_far + w_far * p
                    flux = fluxes(v, v_far, w * w_far, [(q0, far0), (q1, far1)])
                for f, x in enumerate((v, *flux)):
                    edge_value[tile((side * 3 + f) * chunks + c), :] = x

        def level(i, _):
            k = b * BLOCK + i
            over_east = halo_cols[pl.ds(pl.multiple_of(i * ROWS, ROWS), ROWS), :]
            over_west = halo_cols[pl.ds(pl.multiple_of(slab + i * ROWS, ROWS), ROWS), :]
            last = LANES - 1

            def chunk(ref, c):
                return ref[at(k, c), :]

            def edge(side, f, c):
                line = pl.ds(((side * 3 + f) * chunks + c) * ROWS + i, 1)
                return jnp.broadcast_to(edge_value[line, :], (ROWS, LANES))

            def to_last(f):
                return pltpu.roll(over_east, last - f, 1)

            def to_first(f):
                return pltpu.roll(over_west, LANES - f, 1) if f else over_west

            def ahead(turned, c):
                return jnp.where(lane == last, turned[c + 1], turned[c])

            p = [chunk(press, c) for c in range(chunks)]
            w = [chunk(wet, c) for c in range(chunks)]
            p_ahead = [pltpu.roll(x, last, 1) for x in p] + [to_last(4)]
            p_back = [to_first(4)] + [pltpu.roll(x, 1, 1) for x in p]
            u, v = [], []
            for c in range(chunks):
                e, n = chunk(east, c), chunk(pole, c)
                dx = ahead(p_ahead, c) - jnp.where(lane == 0, p_back[c], p_back[c + 1])
                u.append(w[c] * (e + (spin_half * n - dx)))
                dy = pltpu.roll(p[c], ROWS - 1, 0) - pltpu.roll(p[c], 1, 0)
                inside = w[c] * (n - (spin_half * e + dy))
                v.append(jnp.where(row == 0, edge(0, 0, c), jnp.where(row == ROWS - 1, edge(1, 0, c), inside)))
                east_out[at(k, c), :] = u[c]
                pole_out[at(k, c), :] = v[c]

            q = [[chunk(f, c) for c in range(chunks)] for f in (heat, salt)]
            w_ahead = [pltpu.roll(x, last, 1) for x in w] + [to_last(2)]
            u_ahead = [pltpu.roll(x, last, 1) for x in u]
            u_ahead.append(to_last(3) + to_last(2) * p[chunks - 1])
            q_ahead = [
                [pltpu.roll(x, last, 1) for x in q[t]] + [to_last(t)] for t in range(2)
            ]
            w_out = to_first(2)
            u_out = to_first(3) - w_out * p[0]
            flux_back = fluxes(
                u_out, u[0], w_out * w[0], [(to_first(t), q[t][0]) for t in range(2)]
            )
            for c in range(chunks):
                flux = fluxes(
                    u[c],
                    ahead(u_ahead, c),
                    w[c] * ahead(w_ahead, c),
                    [(q[t][c], ahead(q_ahead[t], c)) for t in range(2)],
                )
                turned = [pltpu.roll(x, 1, 1) for x in flux]
                flux_n = fluxes(
                    v[c],
                    pltpu.roll(v[c], ROWS - 1, 0),
                    w[c] * pltpu.roll(w[c], ROWS - 1, 0),
                    [(q[t][c], pltpu.roll(q[t][c], ROWS - 1, 0)) for t in range(2)],
                )
                both = VERT * (w[c] * wet[at(k + 1, c), :])
                for t, (f, out) in enumerate(((heat, heat_out), (salt, salt_out))):
                    above_q = f[at(k + 1, c), :]
                    rise = both * (above_q - q[t][c])
                    held = slice((t * chunks + c) * ROWS, (t * chunks + c + 1) * ROWS)
                    gain = rise - upward[held, :]
                    upward[held, :] = rise
                    dx = flux[t] - jnp.where(lane == 0, flux_back[t], turned[t])
                    over = jnp.where(row == ROWS - 1, edge(1, t + 1, c), flux_n[t])
                    dy = over - jnp.where(row == 0, edge(0, t + 1, c), pltpu.roll(flux_n[t], 1, 0))
                    out[at(k, c), :] = w[c] * ((q[t][c] + gain) - (dx + dy))
                flux_back = turned
            return 0

        lax.fori_loop(0, BLOCK, level, 0)

        groups = chunks // 4
        half = groups * 4 * ROWS
        for c in range(chunks):
            g, across = c // 4, slice((c % 4) * LANES, (c % 4 + 1) * LANES)
            for t, f in enumerate((heat_out, salt_out)):
                x = [f[at(b * BLOCK + i, c), :] for i in range(BLOCK)]
                add = [x[i] + x[BLOCK - 1 - i] for i in range(BLOCK // 2)]
                dif = [WAVE[i] * (x[i] - x[BLOCK - 1 - i]) for i in range(BLOCK // 2)]
                both = jnp.concatenate([FLAT * pairwise_sum(add), pairwise_sum(dif)], 0)
                high = both.astype(jnp.bfloat16)
                base = (g * 2 + t) * 2 * ROWS
                stack[base : base + 2 * ROWS, across] = high
                stack[half + base : half + base + 2 * ROWS, across] = (both - high.astype(jnp.float32)).astype(jnp.bfloat16)
        wide = jnp.dot(stack[...], lane_table[...], preferred_element_type=jnp.float32)
        short = (wide[:half, :LANES] + wide[half:, :LANES]) + (wide[:half, LANES:] + wide[half:, LANES:])
        for g in range(groups):
            for t in range(2):
                for p in range(2):
                    base = ((g * 2 + t) * 2 + p) * ROWS
                    z = short[base : base + ROWS, :]
                    flat, wave = FLAT * z, row_wave * z
                    z = jnp.where(row < 4, flat + pltpu.roll(flat, 4, 0), wave + pltpu.roll(wave, 4, 0))
                    z = z + pltpu.roll(z, 2, 0)
                    z = z + pltpu.roll(z, 1, 0)
                    z = jnp.where(row == 0, pltpu.roll(z, 5, 0), pltpu.roll(z, 2, 0))
                    coef_send[b, t, p, :, g * LANES : (g + 1) * LANES] = z[0:2, :].astype(jnp.bfloat16)
        coef_copy(b, 0).start()
        for dy in turns:
            coef_copy(b, 1, dy).start()

        @pl.when(b == blocks - 1)
        def _():
            for dy in turns:
                coef_copy(b, 3, dy).start()

        coef_keep(b).start()

        @pl.when(b > 0)
        def _():
            coef_copy(b - 1, 0).wait_recv()
            for dy in turns:
                coef_copy(b - 1, 2, dy).start()

        return 0

    lax.fori_loop(0, blocks, second, 0)

    coef_copy(blocks - 1, 0).wait_recv()

    def settle(ref, sem):
        pltpu.make_async_copy(ref, ref, sem).wait()

    settle(coef_out.at[:, :, :, pl.ds(0, width * (n_lon - 2))], coef_sem)
    settle(coef_out.at[:, :, :, pl.ds(0, width * (n_lon - 1))], coef_send_sem)
    settle(coef_send, coef_keep_sem)
    settle(side_send, side_send_sem.at[0])
    settle(side_send, side_send_sem.at[1])

    @pl.when(has_below)
    def _():
        settle(row_send.at[0], row_send_sem.at[0])

    @pl.when(has_above)
    def _():
        settle(row_send.at[1], row_send_sem.at[1])


def deliver_kernel(pieces, *refs):
    count = len(refs) // 2
    sources, places, sem = refs[:count], refs[count : 2 * count], refs[-1]
    copies = []
    for i, (source, target) in enumerate(zip(sources, places)):
        parts = pieces if source.shape[0] % (8 * pieces) == 0 else 1
        size = source.shape[0] // parts
        for p in range(parts):
            part = pl.ds(p * size, size)
            copies.append(pltpu.make_async_copy(source.at[part], target.at[part], sem.at[i, p]))
    for copy in copies:
        copy.start()
    for copy in copies:
        copy.wait()


def deliver(arrays, pieces=4):
    return pl.pallas_call(
        functools.partial(deliver_kernel, pieces),
        out_shape=[pltpu.HBM(x.shape, x.dtype) for x in arrays],
        in_specs=[pl.BlockSpec(memory_space=pltpu.VMEM)] * len(arrays),
        out_specs=[pl.BlockSpec(memory_space=pl.ANY)] * len(arrays),
        scratch_shapes=[pltpu.SemaphoreType.DMA((len(arrays), pieces))],
        compiler_params=pltpu.CompilerParams(vmem_limit_bytes=1 << 20),
        name="deliver",
    )(*(pltpu.with_memory_space_constraint(x, pltpu.VMEM) for x in arrays))


def on_device(n_lat, n_lon, heat, salt, east, pole, spin, sea, depth):
    levels, rows, cols = heat.shape
    chunks, blocks = cols // LANES, levels // BLOCK
    tall = chunks * rows
    total = levels * tall
    field = pltpu.VMEM((total, LANES), jnp.float32)
    longer = pltpu.VMEM((total + tall, LANES), jnp.float32)
    dma = pltpu.SemaphoreType.DMA
    hbm = pl.BlockSpec(memory_space=pl.ANY)

    def tiled(x):
        x = x.reshape(x.shape[:-1] + (chunks, LANES))
        return jnp.swapaxes(x, -3, -2).reshape(-1, LANES)

    def whole(x):
        return jnp.swapaxes(x.reshape(levels, chunks, rows, LANES), 1, 2).reshape(levels, rows, cols)

    outs = pl.pallas_call(
        functools.partial(step_kernel, n_lat, n_lon),
        out_shape=[pltpu.VMEM((total, LANES), jnp.float32)] * 4
        + [pltpu.VMEM((2, 2 * blocks, 2, n_lon * cols // 4), jnp.bfloat16)],
        in_specs=[hbm] * 7,
        out_specs=[pl.BlockSpec(memory_space=pltpu.VMEM)] * 5,
        scratch_shapes=[
            longer,
            longer,
            field,
            field,
            pltpu.VMEM((total, LANES), jnp.int32),
            pltpu.VMEM((tall, LANES), jnp.int32),
            longer,
            field,
            pltpu.VMEM((2, blocks, 4 * BLOCK, cols), jnp.bfloat16),
            pltpu.VMEM((blocks, 4 * BLOCK, cols), jnp.bfloat16),
            pltpu.VMEM((blocks, 4 * BLOCK, cols), jnp.bfloat16),
            pltpu.VMEM((LANES, LANES), jnp.float32),
            pltpu.VMEM((blocks, ROWS, LANES), jnp.float32),
            pltpu.VMEM((blocks, ROWS, LANES), jnp.float32),
            pltpu.VMEM((blocks, ROWS, LANES), jnp.float32),
            pltpu.VMEM((LANES, LANES), jnp.float32),
            pltpu.VMEM((LANES, LANES), jnp.float32),
            pltpu.VMEM((2 * tall, LANES), jnp.float32),
            pltpu.VMEM((tall, LANES), jnp.float32),
            pltpu.VMEM((2 * tall, LANES), jnp.float32),
            pltpu.VMEM((blocks * 2 * 5 * tall, LANES), jnp.float32),
            pltpu.VMEM((2 * 3 * tall, LANES), jnp.float32),
            pltpu.VMEM((4 * LANES, 2 * LANES), jnp.bfloat16),
            pltpu.VMEM((chunks // 4 * 8 * ROWS, 4 * LANES), jnp.bfloat16),
            pltpu.VMEM((blocks, 2, 2, 2, cols // 4), jnp.bfloat16),
            pltpu.SMEM((rows,), jnp.float32),
            dma((blocks,)),
            dma,
            dma,
            dma((2,)),
            dma((blocks,)),
            dma((blocks,)),
            dma((2,)),
            dma((blocks,)),
            dma((blocks,)),
            dma,
            dma,
            dma((blocks,)),
            dma,
        ],
        compiler_params=pltpu.CompilerParams(collective_id=0, has_side_effects=True, vmem_limit_bytes=28 << 20),
        name="ocean_step",
    )(
        *(
            pltpu.with_memory_space_constraint(x, pltpu.HBM)
            for x in (spin, tiled(heat), tiled(salt), tiled(east), tiled(pole), tiled(sea), tiled(depth))
        )
    )
    outs = deliver(outs)
    return tuple(whole(x) for x in outs[:4]) + (outs[4],)


def solution(mesh):
    field = P(None, "lat", "lon")
    return jax.shard_map(
        functools.partial(on_device, mesh.shape["lat"], mesh.shape["lon"]),
        mesh=mesh,
        in_specs=(field, field, field, field, P("lat"), field, P("lat", "lon")),
        out_specs=(field, field, field, field, P(None, None, "lat", None)),
        check_vma=False,
    )
```

time: 57 us -> 35.9 us (0.63)
  the two profiles are of different devices: /device:TPU:0 before, /device:TPU:32 now
where the time goes in v1:
time: 35.9 us; the launch traced here: 35.8 us
  Pallas kernels  35.1 us (98%)
  between operations  0.64 us (2%)
    pallas_call x1, Pallas kernels, on_device(): pl.pallas_call(functools.partial(step_kernel, n_lat, n_lon), out_shape=[p...  31.8 us
    pallas_call x1, Pallas kernels, deliver(): pl.pallas_call(functools.partial(deliver_kernel, pieces), out_shape=[pltp...  3.36 us

profile of v1, /device:TPU:32, one launch (start us, length us, event | category | flops | bytes accessed | tf_op | source)
XLA Modules:
  0.0 35.8 jit_solution(3589903107141370610)
XLA Ops:
  0.6 31.8 %ocean_step.1 = (f32[3840,128]{1,0:T(8,128)S(1)}, f32[3840,128]{1,0:T(8,128)S(1)}, f32[3840,128]{1,0:T(8,128)S(1)}, f32[3840,128]{1,0:T(8,128)S(1)}, bf16[2,10,2,3072]{3,2,1,0:T(2,128)(2,1)S(1)}) custom-call(f32[8]{0:T(128)} %spin_hbm.1, f32[3840,128]{1,0:T(8,128)} %bitcast.50, f32[3840,128]{1,0:T(8,128)} %bitcast.51, f32[3840,128]{1,0:T(8,128)} %bitcast.52, ...), custom_call_target="tpu_custom_call" | custom-call | tf_op jit(solution)/shard_map/ocean_step/pallas_call | solution.py:526
  32.4 3.4 %deliver.1 = (f32[3840,128]{1,0:T(8,128)}, f32[3840,128]{1,0:T(8,128)}, f32[3840,128]{1,0:T(8,128)}, f32[3840,128]{1,0:T(8,128)}, bf16[2,10,2,3072]{3,2,1,0:T(2,128)(2,1)}) custom-call(f32[3840,128]{1,0:T(8,128)S(1)} %get-tuple-element.15.refs_0_, f32[3840,128]{1,0:T(8,128)S(1)} %get-tuple-element.16.refs_1_, f32[3840,128]{1,0:T(8,128)S(1)} %get-tuple-element.17.refs_2_, ...), custom_call_target="tpu_custom_call" | custom-call | tf_op jit(solution)/shard_map/deliver/pallas_call | solution.py:498

commit v2 on v1

--- a/solution.py
+++ b/solution.py
@@ -21,6 +21,17 @@
 BLOCK = 8
 
 
+def once(make):
+    made = {}
+
+    def get(c):
+        if c not in made:
+            made[c] = make(c)
+        return made[c]
+
+    return get
+
+
 def pairwise_sum(parts):
     while len(parts) > 1:
         parts = [sum(parts[i : i + 2][1:], parts[i]) for i in range(0, len(parts), 2)]
@@ -42,6 +53,18 @@
 
 
 REVERSED = (0, 4, 2, 6, 1, 5, 3, 7)
+
+
+AT_ONCE = 2
+
+
+def several(level, count):
+    def turn(i, _):
+        for j in range(count):
+            level(i * count + j)
+        return 0
+
+    lax.fori_loop(0, BLOCK // count, turn, 0)
 
 
 def edge_rows(x, row):
@@ -88,6 +111,7 @@
     halo_box,
     halo_cols,
     upward,
+    side_flux,
     below_sum,
     tower,
     own_edge,
@@ -107,7 +131,6 @@
     east_sem,
     coef_send_sem,
     coef_sem,
-    partner_sem,
     coef_keep_sem,
 ):
     chunks = depth.shape[0] // ROWS
@@ -115,7 +138,6 @@
     tall = chunks * ROWS
     total = press.shape[0]
     blocks = total // (tall * BLOCK)
-    slab = BLOCK * ROWS
     la = lax.axis_index("lat")
     lo = lax.axis_index("lon")
     above = {"lat": lax.rem(la + 1, n_lat)}
@@ -145,6 +167,7 @@
         for i in range(len(fields)):
             load(i, b).start()
 
+    last = LANES - 1
     lane = lax.broadcasted_iota(jnp.int32, (ROWS, LANES), 1)
     row = lax.broadcasted_iota(jnp.int32, (ROWS, LANES), 0)
     zero = jnp.zeros((ROWS, LANES), jnp.float32)
@@ -178,7 +201,6 @@
     for j in range(1, ROWS):
         spin_half = jnp.where(row == j, 0.5 * spin[j], spin_half)
     depth_load.wait()
-    pl.semaphore_wait(barrier, len(peers))
 
     def at(k, c):
         return pl.ds(pl.multiple_of(k * tall, tall) + c * ROWS, ROWS)
@@ -199,6 +221,15 @@
             device_id_type=MESH,
         )
 
+    def send_rows(b):
+        @pl.when(has_below)
+        def _():
+            row_copy(b, 0).start()
+
+        @pl.when(has_above)
+        def _():
+            row_copy(b, 1).start()
+
     def side_copy(b, side):
         return pltpu.make_async_remote_copy(
             src_ref=side_send.at[b],
@@ -209,31 +240,24 @@
             device_id_type=MESH,
         )
 
-    partner = lo + 1 - 2 * lax.rem(lo, 2)
     width = cols // 4
 
     def place(owner):
         return pl.ds(pl.multiple_of(owner * width, LANES), width)
 
-    def coef_copy(b, kind, dy=0):
-        ahead_y = lax.rem(lo + 2 * dy, n_lon)
-        target = (partner, ahead_y, ahead_y, lax.rem(partner + 2 * dy, n_lon))[kind]
-        owner = partner if kind == 2 else lo
-        there = coef_out.at[:, pl.ds(2 * b, 2), :, place(owner)]
+    def coef_copy(b, d):
         return pltpu.make_async_remote_copy(
-            src_ref=there if kind == 2 else coef_send.at[b],
-            dst_ref=there,
+            src_ref=coef_send.at[b],
+            dst_ref=coef_out.at[:, pl.ds(2 * b, 2), :, place(lo)],
             send_sem=coef_send_sem,
-            recv_sem=partner_sem.at[b] if kind == 0 else coef_sem,
-            device_id={"lon": target},
+            recv_sem=coef_sem,
+            device_id={"lon": lax.rem(lo + d, n_lon)},
             device_id_type=MESH,
         )
 
     def coef_keep(b):
         here = coef_out.at[:, pl.ds(2 * b, 2), :, place(lo)]
         return pltpu.make_async_copy(coef_send.at[b], here, coef_keep_sem)
-
-    turns = range(1, n_lon // 2)
 
     def first(b, _):
         pltpu.make_async_copy(heat_hbm, heat.at[pl.ds(0, total)], load_sem.at[b]).wait()
@@ -263,43 +287,126 @@
                     pair = jnp.concatenate([edges[f][side], edges[f + 1][side]], 0)
                     row_send[side, b, 8 * f : 8 * f + 16, ch] = pair.astype(jnp.bfloat16)
 
-        @pl.when(has_below)
+        for i in range(BLOCK):
+            k = b * BLOCK + i
+
+            def ends(get):
+                return jnp.where(lane == 0, get(at(k, 0)), get(at(k, chunks - 1)))
+
+            p = [press[at(k, c), :] for c in (0, chunks - 1)]
+            slope = jnp.where(lane == 0, -pltpu.roll(p[0], last, 1), pltpu.roll(p[1], 1, 1))
+            w = ends(lambda x: wet[x, :])
+            part = w * (ends(lambda x: east[x, :] + spin_half * pole[x, :]) + slope)
+            box = zero
+            values = (ends(lambda x: heat[x, :]), ends(lambda x: salt[x, :]), w, part, jnp.where(lane == 0, *p))
+            for f, v in enumerate(values):
+                box = jnp.where((lane == 2 * f) | (lane == 2 * f + 1), pltpu.roll(v, 2 * f + 1, 1), box)
+            edge_box[i * ROWS : (i + 1) * ROWS, :] = box
+        side_send[b] = edge_box[...].T[: 2 * ROWS, :]
+        @pl.when(b == 0)
         def _():
-            row_copy(b, 0).start()
-
-        @pl.when(has_above)
-        def _():
-            row_copy(b, 1).start()
-
-        for i in range(BLOCK):
-            for side in range(2):
-                here = at(b * BLOCK + i, 0 if side == 0 else chunks - 1)
-                p = press[here, :]
-                w = wet[here, :]
-                flow = east[here, :] + spin_half * pole[here, :]
-                if side == 0:
-                    part = w * (flow - pltpu.roll(p, LANES - 1, 1))
-                else:
-                    part = w * (flow + pltpu.roll(p, 1, 1))
-                box = zero
-                for f, v in enumerate((heat[here, :], salt[here, :], w, part, p)):
-                    shift = f if side == 0 else f + 1
-                    v = pltpu.roll(v, shift, 1) if shift else v
-                    box = jnp.where(lane == f, v, box)
-                edge_box[side * slab + i * ROWS : side * slab + (i + 1) * ROWS, :] = box
-        side_send[b] = edge_box[...].T[:ROWS, :]
+            pl.semaphore_wait(barrier, len(peers))
+
         side_copy(b, 0).start()
         side_copy(b, 1).start()
+
+        @pl.when(b == 0)
+        def _():
+            send_rows(0)
+
+        @pl.when(b == blocks - 2)
+        def _():
+            send_rows(1)
+
         return 0
 
     lax.fori_loop(0, blocks, first, 0)
+    for b in range(2, blocks):
+        send_rows(b)
 
     def second(b, _):
         side_copy(b, 0).wait_recv()
         side_copy(b, 1).wait_recv()
-        halo_box[0:ROWS, :] = jnp.where(lane < slab, from_east[b], from_west[b])
+        odd = lax.rem(lax.broadcasted_iota(jnp.int32, (2 * ROWS, LANES), 0), 2) == 1
+        halo_box[0 : 2 * ROWS, :] = jnp.where(odd, from_east[b], from_west[b])
         halo_cols[...] = halo_box[...].T
 
+        def halo(i):
+            beyond = halo_cols[tile(i), :]
+
+            def to_last(f):
+                return pltpu.roll(beyond, last - (2 * f + 1), 1)
+
+            def to_first(f):
+                return pltpu.roll(beyond, LANES - 2 * f, 1) if f else beyond
+
+            return to_last, to_first
+
+        def ahead(turned, c):
+            return jnp.where(lane == last, turned[c + 1], turned[c])
+
+        def flow(i):
+            k = b * BLOCK + i
+            to_last, to_first = halo(i)
+            p = [press[at(k, c), :] for c in range(chunks)]
+            p_turn = [pltpu.roll(x, last, 1) for x in p] + [to_last(4)]
+            p_back = [to_first(4)] + [pltpu.roll(x, 1, 1) for x in p]
+            for c in range(chunks):
+                here = at(k, c)
+                dx = ahead(p_turn, c) - jnp.where(lane == 0, p_back[c], p_back[c + 1])
+                east_out[here, :] = wet[here, :] * (east[here, :] + (spin_half * pole[here, :] - dx))
+
+        def flux(i):
+            k = b * BLOCK + i
+            to_last, to_first = halo(i)
+            u, w, t, q = ([f[at(k, c), :] for c in range(chunks)] for f in (east_out, wet, heat, salt))
+            u_beyond = to_last(3) + to_last(2) * press[at(k, chunks - 1), :]
+            u_turn, w_turn, t_turn, q_turn = (
+                [pltpu.roll(x, last, 1) for x in f] + [beyond]
+                for f, beyond in ((u, u_beyond), (w, to_last(2)), (t, to_last(0)), (q, to_last(1)))
+            )
+            w_out = to_first(2)
+            u_out = to_first(3) - w_out * press[at(k, 0), :]
+            out = fluxes(u_out, u[0], w_out * w[0], [(to_first(0), t[0]), (to_first(1), q[0])])
+            for f in range(2):
+                side_flux[spot(i, f, -1), :] = out[f]
+            for c in range(chunks):
+                out = fluxes(
+                    u[c], ahead(u_turn, c), w[c] * ahead(w_turn, c), [(t[c], ahead(t_turn, c)), (q[c], ahead(q_turn, c))]
+                )
+                for f in range(2):
+                    side_flux[spot(i, f, c), :] = out[f]
+
+        def spot(i, f, c):
+            return tile((i * 2 + f) * (chunks + 1) + c + 1)
+
+        def gather(i):
+            k = b * BLOCK + i
+            x = [[side_flux[spot(i, f, c), :] for c in range(-1, chunks)] for f in range(2)]
+            back = [[y[0]] + [pltpu.roll(z, 1, 1) for z in y[1:]] for y in x]
+            for c in range(chunks):
+                both = VERT * (wet[at(k, c), :] * wet[at(k + 1, c), :])
+                for f, (field, out) in enumerate(((heat, heat_out), (salt, salt_out))):
+                    q = field[at(k, c), :]
+                    rise = both * (field[at(k + 1, c), :] - q)
+                    held = slice((f * chunks + c) * ROWS, (f * chunks + c + 1) * ROWS)
+                    gain = rise - upward[held, :]
+                    upward[held, :] = rise
+                    dx = x[f][c + 1] - jnp.where(lane == 0, back[f][c], back[f][c + 1])
+                    out[at(k, c), :] = (q + gain) - dx
+
+        for i in range(BLOCK + 2):
+            if i < BLOCK:
+                flow(i)
+            if 0 < i <= BLOCK:
+                flux(i - 1)
+            if i > 1:
+                gather(i - 2)
+        return 0
+
+    lax.fori_loop(0, blocks, second, 0)
+
+    def third(b, _):
         for side in range(2):
             got = from_south if side == 0 else from_north
 
@@ -332,84 +439,33 @@
                 for f, x in enumerate((v, *flux)):
                     edge_value[tile((side * 3 + f) * chunks + c), :] = x
 
-        def level(i, _):
+        def level(i):
             k = b * BLOCK + i
-            over_east = halo_cols[pl.ds(pl.multiple_of(i * ROWS, ROWS), ROWS), :]
-            over_west = halo_cols[pl.ds(pl.multiple_of(slab + i * ROWS, ROWS), ROWS), :]
-            last = LANES - 1
-
-            def chunk(ref, c):
-                return ref[at(k, c), :]
 
             def edge(side, f, c):
                 line = pl.ds(((side * 3 + f) * chunks + c) * ROWS + i, 1)
                 return jnp.broadcast_to(edge_value[line, :], (ROWS, LANES))
 
-            def to_last(f):
-                return pltpu.roll(over_east, last - f, 1)
-
-            def to_first(f):
-                return pltpu.roll(over_west, LANES - f, 1) if f else over_west
-
-            def ahead(turned, c):
-                return jnp.where(lane == last, turned[c + 1], turned[c])
-
-            p = [chunk(press, c) for c in range(chunks)]
-            w = [chunk(wet, c) for c in range(chunks)]
-            p_ahead = [pltpu.roll(x, last, 1) for x in p] + [to_last(4)]
-            p_back = [to_first(4)] + [pltpu.roll(x, 1, 1) for x in p]
-            u, v = [], []
             for c in range(chunks):
-                e, n = chunk(east, c), chunk(pole, c)
-                dx = ahead(p_ahead, c) - jnp.where(lane == 0, p_back[c], p_back[c + 1])
-                u.append(w[c] * (e + (spin_half * n - dx)))
-                dy = pltpu.roll(p[c], ROWS - 1, 0) - pltpu.roll(p[c], 1, 0)
-                inside = w[c] * (n - (spin_half * e + dy))
-                v.append(jnp.where(row == 0, edge(0, 0, c), jnp.where(row == ROWS - 1, edge(1, 0, c), inside)))
-                east_out[at(k, c), :] = u[c]
-                pole_out[at(k, c), :] = v[c]
-
-            q = [[chunk(f, c) for c in range(chunks)] for f in (heat, salt)]
-            w_ahead = [pltpu.roll(x, last, 1) for x in w] + [to_last(2)]
-            u_ahead = [pltpu.roll(x, last, 1) for x in u]
-            u_ahead.append(to_last(3) + to_last(2) * p[chunks - 1])
-            q_ahead = [
-                [pltpu.roll(x, last, 1) for x in q[t]] + [to_last(t)] for t in range(2)
-            ]
-            w_out = to_first(2)
-            u_out = to_first(3) - w_out * p[0]
-            flux_back = fluxes(
-                u_out, u[0], w_out * w[0], [(to_first(t), q[t][0]) for t in range(2)]
-            )
-            for c in range(chunks):
+                here = at(k, c)
+                p, w = press[here, :], wet[here, :]
+                dy = pltpu.roll(p, ROWS - 1, 0) - pltpu.roll(p, 1, 0)
+                v = w * (pole[here, :] - (spin_half * east[here, :] + dy))
+                v = jnp.where(row == 0, edge(0, 0, c), jnp.where(row == ROWS - 1, edge(1, 0, c), v))
+                pole_out[here, :] = v
+                q = [heat[here, :], salt[here, :]]
                 flux = fluxes(
-                    u[c],
-                    ahead(u_ahead, c),
-                    w[c] * ahead(w_ahead, c),
-                    [(q[t][c], ahead(q_ahead[t], c)) for t in range(2)],
+                    v,
+                    pltpu.roll(v, ROWS - 1, 0),
+                    w * pltpu.roll(w, ROWS - 1, 0),
+                    [(x, pltpu.roll(x, ROWS - 1, 0)) for x in q],
                 )
-                turned = [pltpu.roll(x, 1, 1) for x in flux]
-                flux_n = fluxes(
-                    v[c],
-                    pltpu.roll(v[c], ROWS - 1, 0),
-                    w[c] * pltpu.roll(w[c], ROWS - 1, 0),
-                    [(q[t][c], pltpu.roll(q[t][c], ROWS - 1, 0)) for t in range(2)],
-                )
-                both = VERT * (w[c] * wet[at(k + 1, c), :])
-                for t, (f, out) in enumerate(((heat, heat_out), (salt, salt_out))):
-                    above_q = f[at(k + 1, c), :]
-                    rise = both * (above_q - q[t][c])
-                    held = slice((t * chunks + c) * ROWS, (t * chunks + c + 1) * ROWS)
-                    gain = rise - upward[held, :]
-                    upward[held, :] = rise
-                    dx = flux[t] - jnp.where(lane == 0, flux_back[t], turned[t])
-                    over = jnp.where(row == ROWS - 1, edge(1, t + 1, c), flux_n[t])
-                    dy = over - jnp.where(row == 0, edge(0, t + 1, c), pltpu.roll(flux_n[t], 1, 0))
-                    out[at(k, c), :] = w[c] * ((q[t][c] + gain) - (dx + dy))
-                flux_back = turned
-            return 0
-
-        lax.fori_loop(0, BLOCK, level, 0)
+                for f, out in enumerate((heat_out, salt_out)):
+                    over = jnp.where(row == ROWS - 1, edge(1, f + 1, c), flux[f])
+                    under = jnp.where(row == 0, edge(0, f + 1, c), pltpu.roll(flux[f], 1, 0))
+                    out[here, :] = w * (out[here, :] - (over - under))
+
+        several(level, AT_ONCE)
 
         groups = chunks // 4
         half = groups * 4 * ROWS
@@ -437,33 +493,17 @@
                     z = z + pltpu.roll(z, 1, 0)
                     z = jnp.where(row == 0, pltpu.roll(z, 5, 0), pltpu.roll(z, 2, 0))
                     coef_send[b, t, p, :, g * LANES : (g + 1) * LANES] = z[0:2, :].astype(jnp.bfloat16)
-        coef_copy(b, 0).start()
-        for dy in turns:
-            coef_copy(b, 1, dy).start()
-
-        @pl.when(b == blocks - 1)
-        def _():
-            for dy in turns:
-                coef_copy(b, 3, dy).start()
-
+        for d in sorted(range(1, n_lon), key=lambda d: -min(d, n_lon - d)):
+            coef_copy(b, d).start()
         coef_keep(b).start()
-
-        @pl.when(b > 0)
-        def _():
-            coef_copy(b - 1, 0).wait_recv()
-            for dy in turns:
-                coef_copy(b - 1, 2, dy).start()
-
         return 0
 
-    lax.fori_loop(0, blocks, second, 0)
-
-    coef_copy(blocks - 1, 0).wait_recv()
+    lax.fori_loop(0, blocks, third, 0)
 
     def settle(ref, sem):
         pltpu.make_async_copy(ref, ref, sem).wait()
 
-    settle(coef_out.at[:, :, :, pl.ds(0, width * (n_lon - 2))], coef_sem)
+    settle(coef_out.at[:, :, :, pl.ds(0, width * (n_lon - 1))], coef_sem)
     settle(coef_out.at[:, :, :, pl.ds(0, width * (n_lon - 1))], coef_send_sem)
     settle(coef_send, coef_keep_sem)
     settle(side_send, side_send_sem.at[0])
@@ -542,12 +582,13 @@
             pltpu.VMEM((blocks, 4 * BLOCK, cols), jnp.bfloat16),
             pltpu.VMEM((blocks, 4 * BLOCK, cols), jnp.bfloat16),
             pltpu.VMEM((LANES, LANES), jnp.float32),
-            pltpu.VMEM((blocks, ROWS, LANES), jnp.float32),
-            pltpu.VMEM((blocks, ROWS, LANES), jnp.float32),
-            pltpu.VMEM((blocks, ROWS, LANES), jnp.float32),
+            pltpu.VMEM((blocks, 2 * ROWS, LANES), jnp.float32),
+            pltpu.VMEM((blocks, 2 * ROWS, LANES), jnp.float32),
+            pltpu.VMEM((blocks, 2 * ROWS, LANES), jnp.float32),
             pltpu.VMEM((LANES, LANES), jnp.float32),
             pltpu.VMEM((LANES, LANES), jnp.float32),
             pltpu.VMEM((2 * tall, LANES), jnp.float32),
+            pltpu.VMEM((BLOCK * 2 * (chunks + 1) * ROWS, LANES), jnp.float32),
             pltpu.VMEM((tall, LANES), jnp.float32),
             pltpu.VMEM((2 * tall, LANES), jnp.float32),
             pltpu.VMEM((blocks * 2 * 5 * tall, LANES), jnp.float32),
@@ -567,7 +608,6 @@
             dma((blocks,)),
             dma,
             dma,
-            dma((blocks,)),
             dma,
         ],
         compiler_params=pltpu.CompilerParams(collective_id=0, has_side_effects=True, vmem_limit_bytes=28 << 20),

time: 35.9 us -> 31.5 us (0.88)
  the two profiles are of different devices: /device:TPU:32 before, /device:TPU:1 now
where the time goes in v2:
time: 31.5 us; the launch traced here: 31.4 us
  Pallas kernels  30.7 us (97%)
  between operations  0.64 us (2%)
    pallas_call x1, Pallas kernels, on_device(): pl.pallas_call(functools.partial(step_kernel, n_lat, n_lon), out_shape=[p...  27.4 us
    pallas_call x1, Pallas kernels, deliver(): pl.pallas_call(functools.partial(deliver_kernel, pieces), out_shape=[pltp...  3.36 us

profile of v2, /device:TPU:1, one launch (start us, length us, event | category | flops | bytes accessed | tf_op | source)
XLA Modules:
  0.0 31.4 jit_solution(17900629751069510727)
XLA Ops:
  0.6 27.4 %ocean_step.1 = (f32[3840,128]{1,0:T(8,128)S(1)}, f32[3840,128]{1,0:T(8,128)S(1)}, f32[3840,128]{1,0:T(8,128)S(1)}, f32[3840,128]{1,0:T(8,128)S(1)}, bf16[2,10,2,3072]{3,2,1,0:T(2,128)(2,1)S(1)}) custom-call(f32[8]{0:T(128)} %spin_hbm.1, f32[3840,128]{1,0:T(8,128)} %bitcast.50, f32[3840,128]{1,0:T(8,128)} %bitcast.51, f32[3840,128]{1,0:T(8,128)} %bitcast.52, ...), custom_call_target="tpu_custom_call" | custom-call | tf_op jit(solution)/shard_map/ocean_step/pallas_call | solution.py:566
  28.0 3.4 %deliver.1 = (f32[3840,128]{1,0:T(8,128)}, f32[3840,128]{1,0:T(8,128)}, f32[3840,128]{1,0:T(8,128)}, f32[3840,128]{1,0:T(8,128)}, bf16[2,10,2,3072]{3,2,1,0:T(2,128)(2,1)}) custom-call(f32[3840,128]{1,0:T(8,128)S(1)} %get-tuple-element.15.refs_0_, f32[3840,128]{1,0:T(8,128)S(1)} %get-tuple-element.16.refs_1_, f32[3840,128]{1,0:T(8,128)S(1)} %get-tuple-element.17.refs_2_, ...), custom_call_target="tpu_custom_call" | custom-call | tf_op jit(solution)/shard_map/deliver/pallas_call | solution.py:538

commit v3 on v2

--- a/solution.py
+++ b/solution.py
@@ -105,6 +105,7 @@
     from_south,
     from_north,
     edge_box,
+    turned_box,
     side_send,
     from_west,
     from_east,
@@ -232,7 +233,7 @@
 
     def side_copy(b, side):
         return pltpu.make_async_remote_copy(
-            src_ref=side_send.at[b],
+            src_ref=side_send.at[side, b],
             dst_ref=(from_east if side == 0 else from_west).at[b],
             send_sem=side_send_sem.at[side],
             recv_sem=(east_sem if side == 0 else west_sem).at[b],
@@ -302,7 +303,9 @@
             for f, v in enumerate(values):
                 box = jnp.where((lane == 2 * f) | (lane == 2 * f + 1), pltpu.roll(v, 2 * f + 1, 1), box)
             edge_box[i * ROWS : (i + 1) * ROWS, :] = box
-        side_send[b] = edge_box[...].T[: 2 * ROWS, :]
+        turned_box[...] = edge_box[...].T[: 2 * ROWS, :]
+        for side in range(2):
+            side_send[side, b] = turned_box[pl.ds(1 - side, ROWS, stride=2), :]
         @pl.when(b == 0)
         def _():
             pl.semaphore_wait(barrier, len(peers))
@@ -327,18 +330,18 @@
     def second(b, _):
         side_copy(b, 0).wait_recv()
         side_copy(b, 1).wait_recv()
-        odd = lax.rem(lax.broadcasted_iota(jnp.int32, (2 * ROWS, LANES), 0), 2) == 1
-        halo_box[0 : 2 * ROWS, :] = jnp.where(odd, from_east[b], from_west[b])
+        halo_box[0:ROWS, :] = from_east[b]
+        halo_box[ROWS : 2 * ROWS, :] = from_west[b]
         halo_cols[...] = halo_box[...].T
 
         def halo(i):
             beyond = halo_cols[tile(i), :]
 
             def to_last(f):
-                return pltpu.roll(beyond, last - (2 * f + 1), 1)
+                return pltpu.roll(beyond, last - f, 1)
 
             def to_first(f):
-                return pltpu.roll(beyond, LANES - 2 * f, 1) if f else beyond
+                return pltpu.roll(beyond, LANES - ROWS - f, 1)
 
             return to_last, to_first
 
@@ -506,8 +509,8 @@
     settle(coef_out.at[:, :, :, pl.ds(0, width * (n_lon - 1))], coef_sem)
     settle(coef_out.at[:, :, :, pl.ds(0, width * (n_lon - 1))], coef_send_sem)
     settle(coef_send, coef_keep_sem)
-    settle(side_send, side_send_sem.at[0])
-    settle(side_send, side_send_sem.at[1])
+    settle(side_send.at[0], side_send_sem.at[0])
+    settle(side_send.at[1], side_send_sem.at[1])
 
     @pl.when(has_below)
     def _():
@@ -534,7 +537,7 @@
         copy.wait()
 
 
-def deliver(arrays, pieces=4):
+def deliver(arrays, pieces=1):
     return pl.pallas_call(
         functools.partial(deliver_kernel, pieces),
         out_shape=[pltpu.HBM(x.shape, x.dtype) for x in arrays],
@@ -582,9 +585,10 @@
             pltpu.VMEM((blocks, 4 * BLOCK, cols), jnp.bfloat16),
             pltpu.VMEM((blocks, 4 * BLOCK, cols), jnp.bfloat16),
             pltpu.VMEM((LANES, LANES), jnp.float32),
-            pltpu.VMEM((blocks, 2 * ROWS, LANES), jnp.float32),
-            pltpu.VMEM((blocks, 2 * ROWS, LANES), jnp.float32),
-            pltpu.VMEM((blocks, 2 * ROWS, LANES), jnp.float32),
+            pltpu.VMEM((2 * ROWS, LANES), jnp.float32),
+            pltpu.VMEM((2, blocks, ROWS, LANES), jnp.float32),
+            pltpu.VMEM((blocks, ROWS, LANES), jnp.float32),
+            pltpu.VMEM((blocks, ROWS, LANES), jnp.float32),
             pltpu.VMEM((LANES, LANES), jnp.float32),
             pltpu.VMEM((LANES, LANES), jnp.float32),
             pltpu.VMEM((2 * tall, LANES), jnp.float32),

time: 31.5 us -> 30.8 us (0.978)
  Pallas kernels: 30.7 us -> 30.1 us
    pallas_call x1, Pallas kernels: 27.4 us -> 26.8 us  [on_device(): pl.pallas_call(functools.partial(step_kernel, n_lat, n_lon), out_shape=[p...]
where the time goes in v3:
time: 30.8 us; the launch traced here: 30.7 us
  Pallas kernels  30.1 us (98%)
  between operations  0.64 us (2%)
    pallas_call x1, Pallas kernels, on_device(): pl.pallas_call(functools.partial(step_kernel, n_lat, n_lon), out_shape=[p...  26.8 us
    pallas_call x1, Pallas kernels, deliver(): pl.pallas_call(functools.partial(deliver_kernel, pieces), out_shape=[pltp...  3.27 us

profile of v3, /device:TPU:1, one launch (start us, length us, event | category | flops | bytes accessed | tf_op | source)
XLA Modules:
  0.0 30.7 jit_solution(1361184500641884627)
XLA Ops:
  0.6 26.8 %ocean_step.1 = (f32[3840,128]{1,0:T(8,128)S(1)}, f32[3840,128]{1,0:T(8,128)S(1)}, f32[3840,128]{1,0:T(8,128)S(1)}, f32[3840,128]{1,0:T(8,128)S(1)}, bf16[2,10,2,3072]{3,2,1,0:T(2,128)(2,1)S(1)}) custom-call(f32[8]{0:T(128)} %spin_hbm.1, f32[3840,128]{1,0:T(8,128)} %bitcast.50, f32[3840,128]{1,0:T(8,128)} %bitcast.51, f32[3840,128]{1,0:T(8,128)} %bitcast.52, ...), custom_call_target="tpu_custom_call" | custom-call | tf_op jit(solution)/shard_map/ocean_step/pallas_call | solution.py:569
  27.4 3.3 %deliver.1 = (f32[3840,128]{1,0:T(8,128)}, f32[3840,128]{1,0:T(8,128)}, f32[3840,128]{1,0:T(8,128)}, f32[3840,128]{1,0:T(8,128)}, bf16[2,10,2,3072]{3,2,1,0:T(2,128)(2,1)}) custom-call(f32[3840,128]{1,0:T(8,128)S(1)} %get-tuple-element.15.refs_0_, f32[3840,128]{1,0:T(8,128)S(1)} %get-tuple-element.16.refs_1_, f32[3840,128]{1,0:T(8,128)S(1)} %get-tuple-element.17.refs_2_, ...), custom_call_target="tpu_custom_call" | custom-call | tf_op jit(solution)/shard_map/deliver/pallas_call | solution.py:541

commit v4 on v3

--- a/solution.py
+++ b/solution.py
@@ -409,6 +409,9 @@
 
     lax.fori_loop(0, blocks, second, 0)
 
+    along = range(2, n_lon, 2)
+    crossing = range(1, n_lon, 2)
+
     def third(b, _):
         for side in range(2):
             got = from_south if side == 0 else from_north
@@ -441,6 +444,16 @@
                     flux = fluxes(v, v_far, w * w_far, [(q0, far0), (q1, far1)])
                 for f, x in enumerate((v, *flux)):
                     edge_value[tile((side * 3 + f) * chunks + c), :] = x
+
+        @pl.when(b > 1)
+        def _():
+            for d in crossing:
+                coef_copy(b - 2, d).start()
+
+        @pl.when(b == blocks - 1)
+        def _():
+            for d in crossing:
+                coef_copy(b - 1, d).start()
 
         def level(i):
             k = b * BLOCK + i
@@ -496,8 +509,13 @@
                     z = z + pltpu.roll(z, 1, 0)
                     z = jnp.where(row == 0, pltpu.roll(z, 5, 0), pltpu.roll(z, 2, 0))
                     coef_send[b, t, p, :, g * LANES : (g + 1) * LANES] = z[0:2, :].astype(jnp.bfloat16)
-        for d in sorted(range(1, n_lon), key=lambda d: -min(d, n_lon - d)):
+        for d in along:
             coef_copy(b, d).start()
+
+        @pl.when(b == blocks - 1)
+        def _():
+            for d in crossing:
+                coef_copy(b, d).start()
         coef_keep(b).start()
         return 0
 

time: 30.8 us -> 30.3 us (0.984)
  Pallas kernels: 30.1 us -> 29.5 us
    pallas_call x1, Pallas kernels: 26.8 us -> 26.3 us  [on_device(): pl.pallas_call(functools.partial(step_kernel, n_lat, n_lon), out_shape=[p...]
where the time goes in v4:
time: 30.3 us; the launch traced here: 30.2 us
  Pallas kernels  29.5 us (97%)
  between operations  0.64 us (2%)
    pallas_call x1, Pallas kernels, on_device(): pl.pallas_call(functools.partial(step_kernel, n_lat, n_lon), out_shape=[p...  26.3 us
    pallas_call x1, Pallas kernels, deliver(): pl.pallas_call(functools.partial(deliver_kernel, pieces), out_shape=[pltp...  3.27 us

profile of v4, /device:TPU:1, one launch (start us, length us, event | category | flops | bytes accessed | tf_op | source)
XLA Modules:
  0.0 30.2 jit_solution(9577151039234571659)
XLA Ops:
  0.6 26.3 %ocean_step.1 = (f32[3840,128]{1,0:T(8,128)S(1)}, f32[3840,128]{1,0:T(8,128)S(1)}, f32[3840,128]{1,0:T(8,128)S(1)}, f32[3840,128]{1,0:T(8,128)S(1)}, bf16[2,10,2,3072]{3,2,1,0:T(2,128)(2,1)S(1)}) custom-call(f32[8]{0:T(128)} %spin_hbm.1, f32[3840,128]{1,0:T(8,128)} %bitcast.50, f32[3840,128]{1,0:T(8,128)} %bitcast.51, f32[3840,128]{1,0:T(8,128)} %bitcast.52, ...), custom_call_target="tpu_custom_call" | custom-call | tf_op jit(solution)/shard_map/ocean_step/pallas_call | solution.py:587
  26.9 3.3 %deliver.1 = (f32[3840,128]{1,0:T(8,128)}, f32[3840,128]{1,0:T(8,128)}, f32[3840,128]{1,0:T(8,128)}, f32[3840,128]{1,0:T(8,128)}, bf16[2,10,2,3072]{3,2,1,0:T(2,128)(2,1)}) custom-call(f32[3840,128]{1,0:T(8,128)S(1)} %get-tuple-element.15.refs_0_, f32[3840,128]{1,0:T(8,128)S(1)} %get-tuple-element.16.refs_1_, f32[3840,128]{1,0:T(8,128)S(1)} %get-tuple-element.17.refs_2_, ...), custom_call_target="tpu_custom_call" | custom-call | tf_op jit(solution)/shard_map/deliver/pallas_call | solution.py:559

commit v5 on v4

--- a/solution.py
+++ b/solution.py
@@ -55,7 +55,7 @@
 REVERSED = (0, 4, 2, 6, 1, 5, 3, 7)
 
 
-AT_ONCE = 2
+AT_ONCE = 8
 
 
 def several(level, count):
@@ -64,7 +64,10 @@
             level(i * count + j)
         return 0
 
-    lax.fori_loop(0, BLOCK // count, turn, 0)
+    if count == BLOCK:
+        turn(0, 0)
+    else:
+        lax.fori_loop(0, BLOCK // count, turn, 0)
 
 
 def edge_rows(x, row):
@@ -303,7 +306,7 @@
             for f, v in enumerate(values):
                 box = jnp.where((lane == 2 * f) | (lane == 2 * f + 1), pltpu.roll(v, 2 * f + 1, 1), box)
             edge_box[i * ROWS : (i + 1) * ROWS, :] = box
-        turned_box[...] = edge_box[...].T[: 2 * ROWS, :]
+        turned_box[...] = edge_box[...].T[: 3 * ROWS, :]
         for side in range(2):
             side_send[side, b] = turned_box[pl.ds(1 - side, ROWS, stride=2), :]
         @pl.when(b == 0)
@@ -509,13 +512,13 @@
                     z = z + pltpu.roll(z, 1, 0)
                     z = jnp.where(row == 0, pltpu.roll(z, 5, 0), pltpu.roll(z, 2, 0))
                     coef_send[b, t, p, :, g * LANES : (g + 1) * LANES] = z[0:2, :].astype(jnp.bfloat16)
+        @pl.when(b == blocks - 1)
+        def _():
+            for d in sorted(crossing, key=lambda d: -min(d, n_lon - d)):
+                coef_copy(b, d).start()
+
         for d in along:
             coef_copy(b, d).start()
-
-        @pl.when(b == blocks - 1)
-        def _():
-            for d in crossing:
-                coef_copy(b, d).start()
         coef_keep(b).start()
         return 0
 
@@ -603,7 +606,7 @@
             pltpu.VMEM((blocks, 4 * BLOCK, cols), jnp.bfloat16),
             pltpu.VMEM((blocks, 4 * BLOCK, cols), jnp.bfloat16),
             pltpu.VMEM((LANES, LANES), jnp.float32),
-            pltpu.VMEM((2 * ROWS, LANES), jnp.float32),
+            pltpu.VMEM((3 * ROWS, LANES), jnp.float32),
             pltpu.VMEM((2, blocks, ROWS, LANES), jnp.float32),
             pltpu.VMEM((blocks, ROWS, LANES), jnp.float32),
             pltpu.VMEM((blocks, ROWS, LANES), jnp.float32),

time: 30.3 us -> 30.5 us (level)
  no operation moved by 1% of the time
where the time goes in v5:
time: 30.5 us; the launch traced here: 30.4 us
  Pallas kernels  29.7 us (97%)
  between operations  0.64 us (2%)
    pallas_call x1, Pallas kernels, on_device(): pl.pallas_call(functools.partial(step_kernel, n_lat, n_lon), out_shape=[p...  26.5 us
    pallas_call x1, Pallas kernels, deliver(): pl.pallas_call(functools.partial(deliver_kernel, pieces), out_shape=[pltp...  3.27 us

profile of v5, /device:TPU:1, one launch (start us, length us, event | category | flops | bytes accessed | tf_op | source)
XLA Modules:
  0.0 30.4 jit_solution(9701130864322876525)
XLA Ops:
  0.6 26.5 %ocean_step.1 = (f32[3840,128]{1,0:T(8,128)S(1)}, f32[3840,128]{1,0:T(8,128)S(1)}, f32[3840,128]{1,0:T(8,128)S(1)}, f32[3840,128]{1,0:T(8,128)S(1)}, bf16[2,10,2,3072]{3,2,1,0:T(2,128)(2,1)S(1)}) custom-call(f32[8]{0:T(128)} %spin_hbm.1, f32[3840,128]{1,0:T(8,128)} %bitcast.50, f32[3840,128]{1,0:T(8,128)} %bitcast.51, f32[3840,128]{1,0:T(8,128)} %bitcast.52, ...), custom_call_target="tpu_custom_call" | custom-call | tf_op jit(solution)/shard_map/ocean_step/pallas_call | solution.py:590
  27.1 3.3 %deliver.1 = (f32[3840,128]{1,0:T(8,128)}, f32[3840,128]{1,0:T(8,128)}, f32[3840,128]{1,0:T(8,128)}, f32[3840,128]{1,0:T(8,128)}, bf16[2,10,2,3072]{3,2,1,0:T(2,128)(2,1)}) custom-call(f32[3840,128]{1,0:T(8,128)S(1)} %get-tuple-element.15.refs_0_, f32[3840,128]{1,0:T(8,128)S(1)} %get-tuple-element.16.refs_1_, f32[3840,128]{1,0:T(8,128)S(1)} %get-tuple-element.17.refs_2_, ...), custom_call_target="tpu_custom_call" | custom-call | tf_op jit(solution)/shard_map/deliver/pallas_call | solution.py:562
